TPU v7x, 512 devices: a whole 4x8x8 slice. The times are simulated.
512 devices in a mesh: context: 8 (over z), expert: 32 (over x, y), dp: 2 (over core).
Axes of the slice: x: 4, y: 8, z: 8, core: 2. Of those that a mesh axis runs over, the one named last changes fastest.
Arguments:
- residual: bfloat16 [32768, 1024], P(('dp', 'expert', 'context')), parts along dimension 0, may hold values from -6 to 6
- queries: bfloat16 [32768, 2048], P(('dp', 'expert', 'context')), parts along dimension 0, may hold values from -4.6 to 4.6
- key_vectors: bfloat16 [32768, 256], P(('dp', 'expert', 'context')), parts along dimension 0, may hold values from -5 to 5
- value_vectors: bfloat16 [32768, 256], P(('dp', 'expert', 'context')), parts along dimension 0, may hold values from -5 to 5
- output_weight: bfloat16 [2048, 1024], P('context'), may hold values from -0.875 to 0.875
- norm_gain: float32 [1024], replicated, may hold values from 0.1 to 1.9
- routes: int32 [32768, 8], P(('dp', 'expert', 'context')), parts along dimension 0, may hold values from 0 to 127, all different within a row; in each aligned block of 64 rows (0 to 63, 64 to 127, ...) at most 5 rows name the same one
- gate_levels: int32 [32768, 8], P(('dp', 'expert', 'context')), parts along dimension 0, may hold values from 16 to 96
- expert_in: bfloat16 [256, 1024, 384], P(('context', 'expert')), may hold values from -0.1875 to 0.1875
- expert_out: bfloat16 [256, 192, 1024], P(('context', 'expert')), may hold values from -0.3125 to 0.3125
Outputs:
- layer_out: float32 [32768, 1024], P(('dp', 'expert', 'context')), parts along dimension 0
There are 2 independent parts, one for each index of `dp`. A program takes and returns all parts, laid end to end along the dimension named above; an argument that names none is the same for every part. Nothing has to cross between parts.
Inputs may be any that keep to these rules, and one draw needn't show every extreme that they name: `routes`: in the rows of one device no expert is named more than 5 times, and in every draw some expert reaches 5 in some device's rows; each row names 8 different experts.
All inputs are finite; a program needn't handle non-finite values.
Results may differ from a plain program's by a relative error of at most 0.022.
Values may be sent and summed in bfloat16 or wider, within the bound.
No kernel may reach another device: no remote copies, remote signals or barrier semaphores. Data moves between devices by JAX's collectives and lax.ppermute only.
A program may use at most 192 MiB of HBM per device.

v0:
```python
import math
import jax
import jax.numpy as jnp
import numpy as np
from jax import lax
from jax.sharding import PartitionSpec as P

HD = 128


def expert_apply(gathered, weight_in, weight_out):
    projection = jnp.dot(gathered, weight_in, preferred_element_type=jnp.float32)
    inner_half = weight_in.shape[1] // 2
    activated = (jax.nn.silu(projection[:, :inner_half]) * projection[:, inner_half:]).astype(
        jnp.bfloat16
    )
    return jnp.dot(activated, weight_out, preferred_element_type=jnp.float32).astype(jnp.bfloat16)


def local(
    residual,
    queries,
    key_vectors,
    value_vectors,
    output_weight,
    norm_gain,
    routes,
    gate_levels,
    expert_in,
    expert_out,
):
    context_size = lax.axis_size("context")
    expert_size = lax.axis_size("expert")
    tok_rows, width = residual.shape
    head_count = queries.shape[1] // HD
    key_head_count = key_vectors.shape[1] // HD
    group_size = head_count // key_head_count
    heads_here = head_count // context_size
    keys_here = max(1, heads_here // group_size)
    queries_per_key = min(heads_here, group_size)
    group_rows = tok_rows * context_size
    weight_in = expert_in[0]
    weight_out = expert_out[0]
    head_table = (
        (
            np.arange(context_size)[:, None] * heads_here // group_size
            + np.arange(keys_here)[None, :]
        )
        .reshape(-1)
        .astype(np.int32)
    )
    key_select = key_vectors.reshape(tok_rows, key_head_count, HD)[:, head_table].reshape(
        tok_rows, context_size * keys_here * HD
    )
    value_select = value_vectors.reshape(tok_rows, key_head_count, HD)[:, head_table].reshape(
        tok_rows, context_size * keys_here * HD
    )
    query_local, key_local, value_local = (
        lax.all_to_all(queries, "context", split_axis=1, concat_axis=0, tiled=True),
        lax.all_to_all(key_select, "context", split_axis=1, concat_axis=0, tiled=True),
        lax.all_to_all(value_select, "context", split_axis=1, concat_axis=0, tiled=True),
    )
    own_block = lax.axis_index("expert")
    scaling = 1.0 / math.sqrt(HD)
    to_count = query_local.shape[0]
    query_sets = [
        (
            query_local.reshape(to_count, keys_here, queries_per_key, HD)
            .transpose(1, 0, 2, 3)
            .reshape(keys_here, to_count * queries_per_key, HD),
            own_block * group_rows
            + jnp.arange(group_rows * queries_per_key, dtype=jnp.int32) // queries_per_key,
            (own_block + 1) * group_rows,
        )
    ]
    set_counts = [group_rows]
    initial = tuple(
        (
            (
                jnp.full((keys_here, count * queries_per_key), -1e30, jnp.float32),
                jnp.zeros((keys_here, count * queries_per_key), jnp.float32),
                jnp.zeros((keys_here, count * queries_per_key, HD), jnp.float32),
            )
            for count in set_counts
        )
    )
    start = jnp.int32(0)
    key_piece = lax.all_gather(key_local, "expert", axis=0, tiled=True)
    value_piece = lax.all_gather(value_local, "expert", axis=0, tiled=True)
    piece_rows = key_piece.shape[0]
    key_heads = key_piece.reshape(piece_rows, keys_here, HD).transpose(1, 0, 2)
    value_heads = value_piece.reshape(piece_rows, keys_here, HD).transpose(1, 0, 2)
    key_position = jnp.arange(piece_rows, dtype=jnp.int32)
    updated = []
    for query_set, state in zip(query_sets, initial):
        query_rows, query_position, key_limit = query_set

        def update(inner, query_rows=query_rows, query_position=query_position):
            run_max, run_total, accum = inner
            allowed = (key_position[None, :] <= query_position[:, None])[None]
            scores = (
                jnp.einsum(
                    "grd,gnd->grn", query_rows, key_heads, preferred_element_type=jnp.float32
                )
                * scaling
            )
            masked = jnp.where(allowed, scores, -1e30)
            new_max = jnp.maximum(run_max, jnp.max(masked, axis=2))
            weights = jnp.where(allowed, jnp.exp(masked - new_max[:, :, None]), 0.0)
            run_total = jnp.sum(weights, axis=2)
            accum = jnp.einsum(
                "grn,gnd->grd",
                weights.astype(jnp.bfloat16),
                value_heads,
                preferred_element_type=jnp.float32,
            )
            return (new_max, run_total, accum)

        def unchanged(inner):
            return inner

        updated.append(lax.cond(start < key_limit, update, unchanged, state))
    states = tuple(updated)
    run_max, run_total, accum = states[0]
    result = (accum / run_total[:, :, None]).astype(jnp.bfloat16)
    attention = (
        result.reshape(keys_here, group_rows, queries_per_key, HD)
        .transpose(1, 0, 2, 3)
        .reshape(group_rows, heads_here * HD)
    )
    projected = lax.psum_scatter(
        jnp.dot(attention, output_weight, preferred_element_type=jnp.float32).astype(jnp.bfloat16),
        "context",
        scatter_dimension=0,
        tiled=True,
    ).astype(jnp.float32)
    hidden_state = residual.astype(jnp.float32) + projected
    mean_square = jnp.mean(hidden_state * hidden_state, axis=1, keepdims=True)
    normed = (hidden_state * lax.rsqrt(mean_square + 1e-06) * norm_gain).astype(jnp.bfloat16)
    top_count = routes.shape[1]
    expert_count = expert_size * context_size // 2
    group_experts = expert_size // 2
    capacity = min(tok_rows, max(2, 5 * tok_rows * top_count // (4 * expert_count)))
    slot_count = expert_count * capacity
    flat_routes = routes.reshape(-1)
    expert_hits = (
        flat_routes[:, None] == jnp.arange(expert_count, dtype=jnp.int32)[None, :]
    ).astype(jnp.int32)
    earlier = jnp.cumsum(expert_hits, axis=0) - expert_hits
    target_slot = flat_routes * capacity + jnp.sum(earlier * expert_hits, axis=1)
    placement = (
        target_slot.reshape(tok_rows, top_count)[:, :, None]
        == jnp.arange(slot_count, dtype=jnp.int32)[None, None, :]
    )
    sending = jnp.any(placement, axis=1).astype(jnp.bfloat16)
    outgoing = lax.dot_general(
        sending, normed, (((0,), (0,)), ((), ())), preferred_element_type=jnp.float32
    ).astype(jnp.bfloat16)
    gate_shares = jnp.sum(
        jnp.where(placement, gate_levels[:, :, None].astype(jnp.float32) / 256.0, 0.0), axis=1
    ).astype(jnp.bfloat16)
    arrived = lax.all_to_all(
        outgoing.reshape(context_size, group_experts, capacity, width),
        "context",
        split_axis=0,
        concat_axis=0,
        tiled=True,
    )
    item_count = arrived.shape[2]
    copies = jnp.broadcast_to(
        arrived.transpose(1, 0, 2, 3)[:, None], (group_experts, 2, context_size, item_count, width)
    ).reshape(expert_size, context_size, item_count, width)
    rows_in = lax.all_to_all(copies, "expert", split_axis=0, concat_axis=0, tiled=True)
    partial_out = expert_apply(rows_in.reshape(-1, width), weight_in, weight_out).reshape(
        rows_in.shape
    )
    came_back = lax.all_to_all(partial_out, "expert", split_axis=0, concat_axis=0, tiled=True)
    summed = (
        came_back.reshape(group_experts, 2, context_size, item_count, width)
        .astype(jnp.float32)
        .sum(axis=1)
        .astype(jnp.bfloat16)
    )
    result = summed.transpose(1, 0, 2, 3)
    answers = lax.all_to_all(result, "context", split_axis=0, concat_axis=0, tiled=True)
    moe_sum = jnp.dot(
        gate_shares, answers.reshape(slot_count, width), preferred_element_type=jnp.float32
    )
    return hidden_state + moe_sum


def solution(mesh):
    return jax.shard_map(
        local,
        mesh=mesh,
        in_specs=(
            P(("dp", "expert", "context"), None),
            P(("dp", "expert", "context"), None),
            P(("dp", "expert", "context"), None),
            P(("dp", "expert", "context"), None),
            P("context", None),
            P(),
            P(("dp", "expert", "context"), None),
            P(("dp", "expert", "context"), None),
            P(("context", "expert"), None, None),
            P(("context", "expert"), None, None),
        ),
        out_specs=P(("dp", "expert", "context"), None),
        check_vma=False,
    )
```

profile of v0, /device:TPU:8, one launch (start us, length us, event | category | flops | bytes accessed | tf_op | source)
XLA Modules:
  0.0 555.0 jit_solution(13816407835851833400)
XLA Ops:
  6.5 0.7 pad_clamp_fusion
  7.3 0.8 copy_bitcast_fusion.2
  8.0 0.6 gather_fusion
  8.6 19.3 %all_to_all.68 = bf16[64,8,128]{2,0,1:T(8,128)(2,1)} all-to-all(bf16[64,8,128]{2,0,1:T(8,128)(2,1)S(1)} %bitcast.70), channel_id=1, replica_groups=mesh['context'=8,'expert'=32,'dp'=2] {'context'}, dimensions={1} | all-to-all | bytes 262144 | tf_op jit(solution)/shard_map/all_to_all | solution.py:60
  28.0 0.8 copy_bitcast_fusion.1
  28.8 0.6 gather_fusion.1
  29.3 12.1 %all_to_all.69 = bf16[64,8,128]{2,0,1:T(8,128)(2,1)} all-to-all(bf16[64,8,128]{2,0,1:T(8,128)(2,1)S(1)} %bitcast.69), channel_id=1, replica_groups=mesh['context'=8,'expert'=32,'dp'=2] {'context'}, dimensions={1} | all-to-all | bytes 262144 | tf_op jit(solution)/shard_map/all_to_all | solution.py:61
  41.5 1.7 copy.96
  43.2 3.4 all-to-all-start
  46.6 10.3 %all-to-all-done = bf16[64,8,256]{2,0,1:T(8,128)(2,1)S(1)} async-done(((bf16[64,8,256]{2,0,1:T(8,128)(2,1)}), bf16[64,8,256]{2,0,1:T(8,128)(2,1)S(1)}, u32[]{:S(2)}, u32[]{:S(2)}) %all-to-all-start) | async-done | bytes 262176 | tf_op jit(solution)/shard_map/all_to_all | solution.py:59
  57.0 54.5 %all-gather.3.cloned.1.call-done = bf16[16384,128]{1,0:T(8,128)(2,1)} async-done(((bf16[512,128]{1,0:T(8,128)(2,1)}), bf16[16384,128]{1,0:T(8,128)(2,1)}) %all-gather.3.cloned.1.call-update) | async-done | bytes 4194320 | tf_op jit(solution)/shard_map/all_gather | solution.py:88
  111.5 87.7 %all-gather.5.cloned.1.call-done = bf16[16384,128]{1,0:T(8,128)(2,1)} async-done(((bf16[512,128]{1,0:T(8,128)(2,1)}), bf16[16384,128]{1,0:T(8,128)(2,1)}) %all-gather.5.cloned.1.call-update) | async-done | bytes 4194320 | tf_op jit(solution)/shard_map/all_gather | solution.py:89
  199.3 74.4 %conditional.1 = (f32[1,1024]{1,0:T(1,128)S(1)}, f32[1,1024,128]{2,1,0:T(8,128)S(1)}) conditional(s32[]{:T(128)} %convert_element_type.51, () %tuple.19, (s32[16384]{0:T(1024)S(1)}, s32[]{:T(128)}, s32[1024]{0:T(1024)S(1)}, bf16[8,64,256]{2,1,0:T(8,128)(2,1)S(1)}, bf16[16384,128]{1,0:T(8,128)(2,1)}, /*index=5*/bf16[16384,128]{1,0:T(8,128)(2,1)}) %tuple.32), branch_computations={%region_0.1_spmd, %region_1.4_spmd} | conditional | flops 8858378240 | bytes 211267616 | solution.py:122
  199.3 0.1 reshape.111
  199.4 25.7 %fusion = (f32[1024]{0:T(1024)S(1)}, f32[1024,16384]{1,0:T(8,128)}) fusion(s32[16384]{0:T(1024)S(1)} %get-tuple-element.90, s32[1024]{0:T(1024)S(1)} %fusion.8, bf16[1024,128]{1,0:T(8,128)(2,1)S(1)} %reshape.111, bf16[16384,128]{1,0:T(8,128)(2,1)} %get-tuple-element.94), kind=kOutput, calls=%fused_computation.4 | convolution fusion | flops 4362075136 | bytes 71639040 | tf_op jit(solution)/shard_map/cond/branch_1_fun/grd,gnd->grn/dot_general | solution.py:102
  225.2 26.5 %fusion.5 = f32[1,1024,128]{2,1,0:T(8,128)S(1)} fusion(bf16[16384,128]{1,0:T(8,128)(2,1)} %get-tuple-element.95, f32[1024,16384]{1,0:T(8,128)} %get-tuple-element.113, f32[1024]{0:T(1024)S(1)} %broadcast_maximum_fusion, s32[16384]{0:T(1024)S(1)} %get-tuple-element.90, s32[1024]{0:T(1024)S(1)} %fusion.8), kind=kOutput, calls=%fused_computation.8 | convolution fusion | flops 4395630592 | bytes 71901184 | tf_op jit(solution)/shard_map/cond/branch_1_fun/grn,gnd->grd/dot_general | solution.py:111
  251.6 22.1 %fusion.2 = f32[1024]{0:T(1024)S(1)} fusion(f32[1024,16384]{1,0:T(8,128)} %get-tuple-element.113, f32[1024]{0:T(1024)S(1)} %broadcast_maximum_fusion, s32[16384]{0:T(1024)S(1)} %get-tuple-element.90, s32[1024]{0:T(1024)S(1)} %fusion.8), kind=kLoop, calls=%fused_computation.6 | loop fusion | flops 100662272 | bytes 67186688 | tf_op jit(solution)/shard_map/cond/branch_1_fun/reduce_sum | solution.py:110
  273.8 0.2 divide_convert_fusion
  274.1 1.4 convolution_convert_fusion.2
  275.6 0.1 eq.42
  275.8 0.1 copy.76
  275.9 0.2 fusion.22
  276.2 0.2 fusion.21
  276.7 0.5 fusion.13
  277.2 37.8 %reduce-scatter.2.cloned.1.call-done = bf16[64,1024]{1,0:T(8,128)(2,1)} async-done(((bf16[512,1024]{1,0:T(8,128)(2,1)}), bf16[64,1024]{1,0:T(8,128)(2,1)}) %reduce-scatter.2.cloned.1.call-update) | async-done | bytes 131088 | tf_op jit(solution)/shard_map/reduce_scatter | solution.py:131
  315.0 1.0 multiply_reduce_fusion
  316.1 2.5 convolution_convert_fusion.1
  318.7 2.6 reshape.124
  321.3 0.9 copy.81
  322.2 34.2 %all_to_all.70 = bf16[8,16,5,1024]{3,1,2,0:T(8,128)(2,1)S(1)} all-to-all(bf16[8,16,5,1024]{3,1,2,0:T(8,128)(2,1)S(1)} %copy.81), channel_id=1, replica_groups=mesh['context'=8,'expert'=32,'dp'=2] {'context'}, dimensions={0} | all-to-all | bytes 2621440 | tf_op jit(solution)/shard_map/all_to_all | solution.py:162
  356.4 0.7 copy.82
  357.1 0.3 broadcast_in_dim.54
  357.4 66.3 %all_to_all.71 = bf16[32,8,5,1024]{3,1,2,0:T(8,128)(2,1)S(1)} all-to-all(bf16[32,8,5,1024]{3,1,2,0:T(8,128)(2,1)S(1)} %bitcast.61), channel_id=1, replica_groups=mesh['context'=8,'expert'=32,'dp'=2] {'expert'}, dimensions={0} | all-to-all | bytes 5242880 | tf_op jit(solution)/shard_map/all_to_all | solution.py:173
  423.7 4.0 copy.83
  427.7 4.9 reshape.126
  432.7 1.3 fusion.15
  433.9 0.9 convolution_convert_fusion
  434.8 2.9 reshape.127
  437.7 4.9 copy.84
  442.6 61.2 %all_to_all.72 = bf16[32,8,5,1024]{3,1,2,0:T(8,128)(2,1)S(1)} all-to-all(bf16[32,8,5,1024]{3,1,2,0:T(8,128)(2,1)S(1)} %copy.84), channel_id=1, replica_groups=mesh['context'=8,'expert'=32,'dp'=2] {'expert'}, dimensions={0} | all-to-all | bytes 5242880 | tf_op jit(solution)/shard_map/all_to_all | solution.py:177
  503.8 0.6 bitcast_reduce_fusion
  504.4 1.8 copy.86
  506.2 6.4 %all-to-all-start.6 = ((bf16[8,16,5,1024]{3,1,2,0:T(8,128)(2,1)}), bf16[8,16,5,1024]{3,1,2,0:T(8,128)(2,1)}, u32[]{:S(2)}, u32[]{:S(2)}) async-start(bf16[8,16,5,1024]{3,1,2,0:T(8,128)(2,1)} %copy.86), calls=%async_computation.7 | async-start | bytes 2621440 | tf_op jit(solution)/shard_map/all_to_all | solution.py:185
  512.7 0.5 select_reduce_fusion
  513.2 29.2 %all-to-all-done.6 = bf16[8,16,5,1024]{3,1,2,0:T(8,128)(2,1)} async-done(((bf16[8,16,5,1024]{3,1,2,0:T(8,128)(2,1)}), bf16[8,16,5,1024]{3,1,2,0:T(8,128)(2,1)}, u32[]{:S(2)}, u32[]{:S(2)}) %all-to-all-start.6) | async-done | bytes 1310752 | tf_op jit(solution)/shard_map/all_to_all | solution.py:185
  542.4 2.2 copy.87
  544.6 1.4 reshape.129
  546.1 2.4 convolution_add_fusion
  (46 shorter events, 0.9 us)
Async XLA Ops:
  6.5 426.1 %copy-start = (bf16[1,1024,384]{2,1,0:T(8,128)(2,1)S(1)}, bf16[1,1024,384]{2,1,0:T(8,128)(2,1)}, u32[]{:S(2)}) copy-start(bf16[1,1024,384]{2,1,0:T(8,128)(2,1)} %param.23) | copy-start | bytes 2359300
  6.5 105.0 %all-gather.3.cloned.1.call-start = ((), (), s32[]{:S(2)}) async-start(), calls=%async_computation.8 | async-start | bytes 4325376 | tf_op jit(solution)/shard_map/all_gather | solution.py:88
  28.0 171.3 %all-gather.5.cloned.1.call-start = ((), (), s32[]{:S(2)}) async-start(), calls=%async_computation.9 | async-start | bytes 4325376 | tf_op jit(solution)/shard_map/all_gather | solution.py:89
  43.2 13.8 %all-to-all-start = ((bf16[64,8,256]{2,0,1:T(8,128)(2,1)}), bf16[64,8,256]{2,0,1:T(8,128)(2,1)S(1)}, u32[]{:S(2)}, u32[]{:S(2)}) async-start(bf16[64,8,256]{2,0,1:T(8,128)(2,1)} %bitcast.57), calls=%async_computation | async-start | bytes 524288 | tf_op jit(solution)/shard_map/all_to_all | solution.py:59
  46.6 268.4 %reduce-scatter.2.cloned.1.call-start = ((), (), s32[]{:S(2)}) async-start(), calls=%async_computation.10 | async-start | bytes 1179648 | tf_op jit(solution)/shard_map/reduce_scatter | solution.py:131
  199.3 74.8 %copy-start.3 = (bf16[256,1024]{1,0:T(8,128)(2,1)S(1)}, bf16[256,1024]{1,0:T(8,128)(2,1)}, u32[]{:S(2)}) copy-start(bf16[256,1024]{1,0:T(8,128)(2,1)} %param.19) | copy-start | bytes 1572868
  273.7 1.8 copy-start.6
  273.7 41.3 %copy-start.1 = (bf16[64,1024]{1,0:T(8,128)(2,1)S(1)}, bf16[64,1024]{1,0:T(8,128)(2,1)}, u32[]{:S(2)}) copy-start(bf16[64,1024]{1,0:T(8,128)(2,1)} %param.15) | copy-start | bytes 393220
  273.7 42.4 %copy-start.7 = (f32[1024]{0:T(1024)S(1)}, f32[1024]{0:T(1024)}, u32[]{:S(2)}) copy-start(f32[1024]{0:T(1024)} %param.20) | copy-start | bytes 12292
  276.7 39.4 %copy-start.4 = (s32[64,8]{1,0:T(8,128)}, s32[64,8]{1,0:T(8,128)S(1)}, u32[]{:S(2)}) copy-start(s32[64,8]{1,0:T(8,128)S(1)} %copy.79) | copy-start | bytes 6148
  432.6 1.3 copy-start.9
  503.8 8.8 %copy-start.8 = (s32[64,8]{0,1:T(8,128)S(1)}, s32[64,8]{0,1:T(8,128)}, u32[]{:S(2)}) copy-start(s32[64,8]{0,1:T(8,128)} %param.22) | copy-start | bytes 6148
  503.8 8.9 %copy-start.5 = (s32[64,8]{1,0:T(8,128)S(1)}, s32[64,8]{1,0:T(8,128)}, u32[]{:S(2)}) copy-start(s32[64,8]{1,0:T(8,128)} %copy-done.4) | copy-start | bytes 6148
  506.2 39.9 %copy-start.2 = (bf16[64,1024]{1,0:T(8,128)(2,1)S(1)}, bf16[64,1024]{1,0:T(8,128)(2,1)}, u32[]{:S(2)}) copy-start(bf16[64,1024]{1,0:T(8,128)(2,1)} %reduce-scatter.2.cloned.1.call-done) | copy-start | bytes 393220
  506.2 36.2 %all-to-all-start.6 = ((bf16[8,16,5,1024]{3,1,2,0:T(8,128)(2,1)}), bf16[8,16,5,1024]{3,1,2,0:T(8,128)(2,1)}, u32[]{:S(2)}, u32[]{:S(2)}) async-start(bf16[8,16,5,1024]{3,1,2,0:T(8,128)(2,1)} %copy.86), calls=%async_computation.7 | async-start | bytes 2621440 | tf_op jit(solution)/shard_map/all_to_all | solution.py:185
Sparse Core Ops, SparseCore 0:
  28.1 83.4 all-gather.2
  114.7 84.5 all-gather.4
  275.7 39.3 reduce-scatter.1
where the time goes:
time: 556 us; the launch traced here: 555 us
  waiting for transfers between devices  220 us (40%)
  blocking collectives  193 us (35%)
  matrix products  60.7 us (11%)
  local copies, waits for them, and re-layouts  32 us (6%)
  other arithmetic  26.1 us (5%)
  between operations  13.4 us (2%)
  starting transfers between devices  9.92 us (2%)
    all_gather x1, waiting for transfers between devices, local(): value_piece = lax.all_gather(value_local, 'expert', axis=0, tiled=True)  87.7 us
    all_to_all x1, blocking collectives, local(): lax.all_to_all(copies, 'expert', split_axis=0, concat_axis=0, tiled=True)  66.3 us
    all_to_all x1, blocking collectives, local(): lax.all_to_all(partial_out, 'expert', split_axis=0, concat_axis=0, tiled=...  61.2 us
    all_gather x1, waiting for transfers between devices, local(): key_piece = lax.all_gather(key_local, 'expert', axis=0, tiled=True)  54.5 us
    reduce_scatter x1, waiting for transfers between devices, local(): lax.psum_scatter(jnp.dot(attention, output_weight, preferred_element_type...  37.8 us
    all_to_all x1, blocking collectives, local(): lax.all_to_all(outgoing.reshape(context_size, group_experts, capacity, wi...  34.2 us
    all_to_all x1, waiting for transfers between devices, local(): lax.all_to_all(result, 'context', split_axis=0, concat_axis=0, tiled=True)  29.2 us
    dot_general x1, matrix products, update(): jnp.einsum('grn,gnd->grd', weights.astype(jnp.bfloat16), value_heads, pre...  26.5 us
  transfers between devices with their start and end apart: 5, of which 5 were waited for; matrix products, arithmetic and copies ran while one was open for 1% of the time, Pallas kernels for 0%

commit v1 on v0

--- a/solution.py
+++ b/solution.py
@@ -6,6 +6,29 @@
 from jax.sharding import PartitionSpec as P
 
 HD = 128
+
+
+def cut_along(x, dim, size):
+    dims = x.shape
+    blocks = x.reshape(*dims[:dim], size, dims[dim] // size, *dims[dim + 1 :])
+    return jnp.moveaxis(blocks, dim, 0)
+
+
+def laid_out(pieces, dim):
+    lengths = list(pieces.shape[1:])
+    lengths[dim] *= pieces.shape[0]
+    return jnp.moveaxis(pieces, 0, dim).reshape(lengths)
+
+
+def exchange_in_pairs(value, axis, split_dim, concat_dim):
+    count, index = (lax.axis_size(axis), lax.axis_index(axis))
+    tiles = cut_along(value, split_dim, count)
+    outs = [tiles[index]]
+    for step in range(1, count):
+        sent = tiles[index ^ step]
+        outs.append(lax.ppermute(sent, axis, [(i, i ^ step) for i in range(count)]))
+    tiles = jnp.stack(outs)[index ^ jnp.arange(count)]
+    return laid_out(tiles, concat_dim)
 
 
 def expert_apply(gathered, weight_in, weight_out):
@@ -57,7 +80,7 @@
     )
     query_local, key_local, value_local = (
         lax.all_to_all(queries, "context", split_axis=1, concat_axis=0, tiled=True),
-        lax.all_to_all(key_select, "context", split_axis=1, concat_axis=0, tiled=True),
+        exchange_in_pairs(key_select, "context", 1, 0),
         lax.all_to_all(value_select, "context", split_axis=1, concat_axis=0, tiled=True),
     )
     own_block = lax.axis_index("expert")

time: 556 us -> 576 us (1.036)
  starting transfers between devices: 9.92 us -> 42.3 us
  blocking collectives: 193 us -> 174 us
  waiting for transfers between devices: 220 us -> 226 us
    ppermute x0 -> x7, starting transfers between devices: none -> 32.7 us  [exchange_in_pairs(): outs.append(lax.ppermute(sent, axis, [(i, i ^ step) for i in range(count)]))]
    all_to_all x1 -> x0, blocking collectives: 19.3 us -> none  [local(): lax.all_to_all(key_select, 'context', split_axis=1, concat_axis=0, tiled=...]
  transfers between devices with their start and end apart: 5 -> 12, of which waited for: 5 -> 6; matrix products, arithmetic and copies ran while one was open for 1% -> 1% of each run, Pallas kernels for 0% -> 0%
where the time goes in v1:
time: 576 us; the launch traced here: 575 us
  waiting for transfers between devices  226 us (39%)
  blocking collectives  174 us (30%)
  matrix products  60.6 us (11%)
  starting transfers between devices  42.3 us (7%)
  local copies, waits for them, and re-layouts  33.2 us (6%)
  other arithmetic  26.1 us (5%)
  between operations  13.5 us (2%)
    all_gather x1, waiting for transfers between devices, local(): value_piece = lax.all_gather(value_local, 'expert', axis=0, tiled=True)  87.7 us
    all_to_all x1, blocking collectives, local(): lax.all_to_all(copies, 'expert', split_axis=0, concat_axis=0, tiled=True)  66.3 us
    all_to_all x1, blocking collectives, local(): lax.all_to_all(partial_out, 'expert', split_axis=0, concat_axis=0, tiled=...  61.1 us
    all_gather x1, waiting for transfers between devices, local(): key_piece = lax.all_gather(key_local, 'expert', axis=0, tiled=True)  55.5 us
    reduce_scatter x1, waiting for transfers between devices, local(): lax.psum_scatter(jnp.dot(attention, output_weight, preferred_element_type...  38 us
    all_to_all x1, blocking collectives, local(): lax.all_to_all(outgoing.reshape(context_size, group_experts, capacity, wi...  34.1 us
    ppermute x7, starting transfers between devices, exchange_in_pairs(): outs.append(lax.ppermute(sent, axis, [(i, i ^ step) for i in range(count)]))  32.7 us
    all_to_all x1, waiting for transfers between devices, local(): lax.all_to_all(result, 'context', split_axis=0, concat_axis=0, tiled=True)  29 us
  transfers between devices with their start and end apart: 12, of which 6 were waited for; matrix products, arithmetic and copies ran while one was open for 1% of the time, Pallas kernels for 0%

profile of v1, /device:TPU:8, one launch (start us, length us, event | category | flops | bytes accessed | tf_op | source)
XLA Modules:
  0.0 575.1 jit_solution(10097242134969723054)
XLA Ops:
  6.5 0.7 pad_clamp_fusion.1
  7.3 0.8 copy_bitcast_fusion.2
  8.0 0.6 gather_fusion
  8.7 4.3 collective-permute-start
  12.9 6.1 %collective-permute-start.1 = (bf16[64,128]{1,0:T(8,128)(2,1)S(1)}, bf16[64,128]{1,0:T(8,128)(2,1)S(1)}, u32[]{:S(2)}, u32[]{:S(2)}) collective-permute-start(bf16[64,128]{1,0:T(8,128)(2,1)S(1)} %get-tuple-element.119), channel_id=1, source_target_pairs={{0,128},{64,192},{128,0},{192,64},{256,384},{320,448},{384,256},{4... | collective-permute-start | bytes 49160 | tf_op jit(solution)/shard_map/ppermute | solution.py:29
  19.0 1.9 collective-permute-start.2
  21.0 8.7 %collective-permute-start.3 = (bf16[64,128]{1,0:T(8,128)(2,1)S(1)}, bf16[64,128]{1,0:T(8,128)(2,1)S(1)}, u32[]{:S(2)}, u32[]{:S(2)}) collective-permute-start(bf16[64,128]{1,0:T(8,128)(2,1)S(1)} %get-tuple-element.117), channel_id=1, source_target_pairs={{0,256},{64,320},{128,384},{192,448},{256,0},{320,64},{384,128},{4... | collective-permute-start | bytes 49160 | tf_op jit(solution)/shard_map/ppermute | solution.py:29
  29.7 1.9 collective-permute-start.4
  31.7 7.9 %collective-permute-start.5 = (bf16[64,128]{1,0:T(8,128)(2,1)S(1)}, bf16[64,128]{1,0:T(8,128)(2,1)S(1)}, u32[]{:S(2)}, u32[]{:S(2)}) collective-permute-start(bf16[64,128]{1,0:T(8,128)(2,1)S(1)} %get-tuple-element.115), channel_id=1, source_target_pairs={{0,384},{64,448},{128,256},{192,320},{256,128},{320,192},{384,0},{... | collective-permute-start | bytes 49160 | tf_op jit(solution)/shard_map/ppermute | solution.py:29
  39.6 1.9 collective-permute-start.6
  41.6 5.0 collective-permute-done.6
  46.6 1.2 gather_fusion.1
  47.9 0.8 copy_bitcast_fusion.1
  48.6 0.6 gather_fusion.2
  49.2 12.1 %all_to_all.52 = bf16[64,8,128]{2,0,1:T(8,128)(2,1)} all-to-all(bf16[64,8,128]{2,0,1:T(8,128)(2,1)S(1)} %bitcast.96), channel_id=1, replica_groups=mesh['context'=8,'expert'=32,'dp'=2] {'context'}, dimensions={1} | all-to-all | bytes 262144 | tf_op jit(solution)/shard_map/all_to_all | solution.py:84
  61.4 1.7 copy.96
  63.0 3.4 all-to-all-start
  66.5 10.3 %all-to-all-done = bf16[64,8,256]{2,0,1:T(8,128)(2,1)S(1)} async-done(((bf16[64,8,256]{2,0,1:T(8,128)(2,1)}), bf16[64,8,256]{2,0,1:T(8,128)(2,1)S(1)}, u32[]{:S(2)}, u32[]{:S(2)}) %all-to-all-start) | async-done | bytes 262176 | tf_op jit(solution)/shard_map/all_to_all | solution.py:82
  76.9 55.5 %all-gather.3.cloned.1.call-done = bf16[16384,128]{1,0:T(8,128)(2,1)} async-done(((bf16[512,128]{1,0:T(8,128)(2,1)}), bf16[16384,128]{1,0:T(8,128)(2,1)}) %all-gather.3.cloned.1.call-update) | async-done | bytes 4194320 | tf_op jit(solution)/shard_map/all_gather | solution.py:111
  132.4 87.7 %all-gather.5.cloned.1.call-done = bf16[16384,128]{1,0:T(8,128)(2,1)} async-done(((bf16[512,128]{1,0:T(8,128)(2,1)}), bf16[16384,128]{1,0:T(8,128)(2,1)}) %all-gather.5.cloned.1.call-update) | async-done | bytes 4194320 | tf_op jit(solution)/shard_map/all_gather | solution.py:112
  220.2 74.3 %conditional.1 = (f32[1,1024]{1,0:T(1,128)S(1)}, f32[1,1024,128]{2,1,0:T(8,128)S(1)}) conditional(s32[]{:T(128)} %convert_element_type.51, () %tuple.19, (s32[16384]{0:T(1024)S(1)}, s32[]{:T(128)}, s32[1024]{0:T(1024)S(1)}, bf16[8,64,256]{2,1,0:T(8,128)(2,1)S(1)}, bf16[16384,128]{1,0:T(8,128)(2,1)}, /*index=5*/bf16[16384,128]{1,0:T(8,128)(2,1)}) %tuple.39), branch_computations={%region_0.1_spmd, %region_1.4_spmd} | conditional | flops 8858378240 | bytes 211267616 | solution.py:145
  220.3 25.7 %fusion = (f32[1024]{0:T(1024)S(1)}, f32[1024,16384]{1,0:T(8,128)}) fusion(s32[16384]{0:T(1024)S(1)} %get-tuple-element.90, s32[1024]{0:T(1024)S(1)} %fusion.8, bf16[1024,128]{1,0:T(8,128)(2,1)S(1)} %reshape.139, bf16[16384,128]{1,0:T(8,128)(2,1)} %get-tuple-element.94), kind=kOutput, calls=%fused_computation.5 | convolution fusion | flops 4362075136 | bytes 71639040 | tf_op jit(solution)/shard_map/cond/branch_1_fun/grd,gnd->grn/dot_general | solution.py:125
  246.0 26.5 %fusion.5 = f32[1,1024,128]{2,1,0:T(8,128)S(1)} fusion(bf16[16384,128]{1,0:T(8,128)(2,1)} %get-tuple-element.95, f32[1024,16384]{1,0:T(8,128)} %get-tuple-element.113, f32[1024]{0:T(1024)S(1)} %broadcast_maximum_fusion, s32[16384]{0:T(1024)S(1)} %get-tuple-element.90, s32[1024]{0:T(1024)S(1)} %fusion.8), kind=kOutput, calls=%fused_computation.9 | convolution fusion | flops 4395630592 | bytes 71901184 | tf_op jit(solution)/shard_map/cond/branch_1_fun/grn,gnd->grd/dot_general | solution.py:134
  272.4 22.1 %fusion.2 = f32[1024]{0:T(1024)S(1)} fusion(f32[1024,16384]{1,0:T(8,128)} %get-tuple-element.113, f32[1024]{0:T(1024)S(1)} %broadcast_maximum_fusion, s32[16384]{0:T(1024)S(1)} %get-tuple-element.90, s32[1024]{0:T(1024)S(1)} %fusion.8), kind=kLoop, calls=%fused_computation.7 | loop fusion | flops 100662272 | bytes 67186688 | tf_op jit(solution)/shard_map/cond/branch_1_fun/reduce_sum | solution.py:133
  294.9 1.4 convolution_convert_fusion.2
  298.0 38.0 %reduce-scatter.2.cloned.1.call-done = bf16[64,1024]{1,0:T(8,128)(2,1)} async-done(((bf16[512,1024]{1,0:T(8,128)(2,1)}), bf16[64,1024]{1,0:T(8,128)(2,1)}) %reduce-scatter.2.cloned.1.call-update) | async-done | bytes 131088 | tf_op jit(solution)/shard_map/reduce_scatter | solution.py:154
  335.9 1.0 multiply_reduce_fusion
  337.0 2.6 convolution_convert_fusion.1
  339.6 2.6 reshape.154
  342.2 0.9 copy.81
  343.1 34.1 %all_to_all.53 = bf16[8,16,5,1024]{3,1,2,0:T(8,128)(2,1)S(1)} all-to-all(bf16[8,16,5,1024]{3,1,2,0:T(8,128)(2,1)S(1)} %copy.81), channel_id=1, replica_groups=mesh['context'=8,'expert'=32,'dp'=2] {'context'}, dimensions={0} | all-to-all | bytes 2621440 | tf_op jit(solution)/shard_map/all_to_all | solution.py:185
  377.2 0.7 copy.82
  378.3 66.3 %all_to_all.54 = bf16[32,8,5,1024]{3,1,2,0:T(8,128)(2,1)S(1)} all-to-all(bf16[32,8,5,1024]{3,1,2,0:T(8,128)(2,1)S(1)} %bitcast.88), channel_id=1, replica_groups=mesh['context'=8,'expert'=32,'dp'=2] {'expert'}, dimensions={0} | all-to-all | bytes 5242880 | tf_op jit(solution)/shard_map/all_to_all | solution.py:196
  444.5 4.0 copy.83
  448.6 4.9 reshape.156
  453.5 1.3 fusion.15
  454.8 0.9 convolution_convert_fusion
  455.7 2.8 reshape.157
  458.5 4.9 copy.84
  463.4 61.1 %all_to_all.55 = bf16[32,8,5,1024]{3,1,2,0:T(8,128)(2,1)S(1)} all-to-all(bf16[32,8,5,1024]{3,1,2,0:T(8,128)(2,1)S(1)} %copy.84), channel_id=1, replica_groups=mesh['context'=8,'expert'=32,'dp'=2] {'expert'}, dimensions={0} | all-to-all | bytes 5242880 | tf_op jit(solution)/shard_map/all_to_all | solution.py:200
  524.5 0.6 bitcast_reduce_fusion
  525.1 1.8 copy.86
  526.9 6.0 %all-to-all-start.5 = ((bf16[8,16,5,1024]{3,1,2,0:T(8,128)(2,1)}), bf16[8,16,5,1024]{3,1,2,0:T(8,128)(2,1)}, u32[]{:S(2)}, u32[]{:S(2)}) async-start(bf16[8,16,5,1024]{3,1,2,0:T(8,128)(2,1)} %copy.86), calls=%async_computation.6 | async-start | bytes 2621440 | tf_op jit(solution)/shard_map/all_to_all | solution.py:208
  533.1 0.5 select_reduce_fusion
  533.5 29.0 %all-to-all-done.5 = bf16[8,16,5,1024]{3,1,2,0:T(8,128)(2,1)} async-done(((bf16[8,16,5,1024]{3,1,2,0:T(8,128)(2,1)}), bf16[8,16,5,1024]{3,1,2,0:T(8,128)(2,1)}, u32[]{:S(2)}, u32[]{:S(2)}) %all-to-all-start.5) | async-done | bytes 1310752 | tf_op jit(solution)/shard_map/all_to_all | solution.py:208
  562.6 2.2 copy.87
  564.8 1.4 reshape.159
  566.2 2.4 convolution_add_fusion
  (70 shorter events, 2.8 us)
Async XLA Ops:
  6.5 446.9 %copy-start = (bf16[1,1024,384]{2,1,0:T(8,128)(2,1)S(1)}, bf16[1,1024,384]{2,1,0:T(8,128)(2,1)}, u32[]{:S(2)}) copy-start(bf16[1,1024,384]{2,1,0:T(8,128)(2,1)} %param.23) | copy-start | bytes 2359300
  6.5 125.9 %all-gather.3.cloned.1.call-start = ((), (), s32[]{:S(2)}) async-start(), calls=%async_computation.7 | async-start | bytes 4325376 | tf_op jit(solution)/shard_map/all_gather | solution.py:111
  8.7 23.0 %collective-permute-start = (bf16[64,128]{1,0:T(8,128)(2,1)S(1)}, bf16[64,128]{1,0:T(8,128)(2,1)S(1)}, u32[]{:S(2)}, u32[]{:S(2)}) collective-permute-start(bf16[64,128]{1,0:T(8,128)(2,1)S(1)} %get-tuple-element.120), channel_id=1, source_target_pairs={{0,64},{64,0},{128,192},{192,128},{256,320},{320,256},{384,448},{4... | collective-permute-start | bytes 49160 | tf_op jit(solution)/shard_map/ppermute | solution.py:29
  12.9 26.6 %collective-permute-start.1 = (bf16[64,128]{1,0:T(8,128)(2,1)S(1)}, bf16[64,128]{1,0:T(8,128)(2,1)S(1)}, u32[]{:S(2)}, u32[]{:S(2)}) collective-permute-start(bf16[64,128]{1,0:T(8,128)(2,1)S(1)} %get-tuple-element.119), channel_id=1, source_target_pairs={{0,128},{64,192},{128,0},{192,64},{256,384},{320,448},{384,256},{4... | collective-permute-start | bytes 49160 | tf_op jit(solution)/shard_map/ppermute | solution.py:29
  19.0 22.5 %collective-permute-start.2 = (bf16[64,128]{1,0:T(8,128)(2,1)S(1)}, bf16[64,128]{1,0:T(8,128)(2,1)S(1)}, u32[]{:S(2)}, u32[]{:S(2)}) collective-permute-start(bf16[64,128]{1,0:T(8,128)(2,1)S(1)} %get-tuple-element.118), channel_id=1, source_target_pairs={{0,192},{64,128},{128,64},{192,0},{256,448},{320,384},{384,320},{4... | collective-permute-start | bytes 49160 | tf_op jit(solution)/shard_map/ppermute | solution.py:29
  21.0 20.6 %collective-permute-start.3 = (bf16[64,128]{1,0:T(8,128)(2,1)S(1)}, bf16[64,128]{1,0:T(8,128)(2,1)S(1)}, u32[]{:S(2)}, u32[]{:S(2)}) collective-permute-start(bf16[64,128]{1,0:T(8,128)(2,1)S(1)} %get-tuple-element.117), channel_id=1, source_target_pairs={{0,256},{64,320},{128,384},{192,448},{256,0},{320,64},{384,128},{4... | collective-permute-start | bytes 49160 | tf_op jit(solution)/shard_map/ppermute | solution.py:29
  29.7 11.8 %collective-permute-start.4 = (bf16[64,128]{1,0:T(8,128)(2,1)S(1)}, bf16[64,128]{1,0:T(8,128)(2,1)S(1)}, u32[]{:S(2)}, u32[]{:S(2)}) collective-permute-start(bf16[64,128]{1,0:T(8,128)(2,1)S(1)} %get-tuple-element.116), channel_id=1, source_target_pairs={{0,320},{64,256},{128,448},{192,384},{256,64},{320,0},{384,192},{4... | collective-permute-start | bytes 49160 | tf_op jit(solution)/shard_map/ppermute | solution.py:29
  31.7 9.9 %collective-permute-start.5 = (bf16[64,128]{1,0:T(8,128)(2,1)S(1)}, bf16[64,128]{1,0:T(8,128)(2,1)S(1)}, u32[]{:S(2)}, u32[]{:S(2)}) collective-permute-start(bf16[64,128]{1,0:T(8,128)(2,1)S(1)} %get-tuple-element.115), channel_id=1, source_target_pairs={{0,384},{64,448},{128,256},{192,320},{256,128},{320,192},{384,0},{... | collective-permute-start | bytes 49160 | tf_op jit(solution)/shard_map/ppermute | solution.py:29
  39.6 7.0 %collective-permute-start.6 = (bf16[64,128]{1,0:T(8,128)(2,1)S(1)}, bf16[64,128]{1,0:T(8,128)(2,1)S(1)}, u32[]{:S(2)}, u32[]{:S(2)}) collective-permute-start(bf16[64,128]{1,0:T(8,128)(2,1)S(1)} %get-tuple-element.114), channel_id=1, source_target_pairs={{0,448},{64,384},{128,320},{192,256},{256,192},{320,128},{384,64},... | collective-permute-start | bytes 49160 | tf_op jit(solution)/shard_map/ppermute | solution.py:29
  47.8 172.3 %all-gather.5.cloned.1.call-start = ((), (), s32[]{:S(2)}) async-start(), calls=%async_computation.8 | async-start | bytes 4325376 | tf_op jit(solution)/shard_map/all_gather | solution.py:112
  63.0 13.8 %all-to-all-start = ((bf16[64,8,256]{2,0,1:T(8,128)(2,1)}), bf16[64,8,256]{2,0,1:T(8,128)(2,1)S(1)}, u32[]{:S(2)}, u32[]{:S(2)}) async-start(bf16[64,8,256]{2,0,1:T(8,128)(2,1)} %bitcast.84), calls=%async_computation | async-start | bytes 524288 | tf_op jit(solution)/shard_map/all_to_all | solution.py:82
  66.5 269.5 %reduce-scatter.2.cloned.1.call-start = ((), (), s32[]{:S(2)}) async-start(), calls=%async_computation.9 | async-start | bytes 1179648 | tf_op jit(solution)/shard_map/reduce_scatter | solution.py:154
  220.1 74.7 %copy-start.3 = (bf16[256,1024]{1,0:T(8,128)(2,1)S(1)}, bf16[256,1024]{1,0:T(8,128)(2,1)}, u32[]{:S(2)}) copy-start(bf16[256,1024]{1,0:T(8,128)(2,1)} %param.19) | copy-start | bytes 1572868
  294.5 1.8 copy-start.6
  294.5 41.4 %copy-start.1 = (bf16[64,1024]{1,0:T(8,128)(2,1)S(1)}, bf16[64,1024]{1,0:T(8,128)(2,1)}, u32[]{:S(2)}) copy-start(bf16[64,1024]{1,0:T(8,128)(2,1)} %param.15) | copy-start | bytes 393220
  294.5 42.5 %copy-start.7 = (f32[1024]{0:T(1024)S(1)}, f32[1024]{0:T(1024)}, u32[]{:S(2)}) copy-start(f32[1024]{0:T(1024)} %param.20) | copy-start | bytes 12292
  297.5 39.5 %copy-start.4 = (s32[64,8]{1,0:T(8,128)}, s32[64,8]{1,0:T(8,128)S(1)}, u32[]{:S(2)}) copy-start(s32[64,8]{1,0:T(8,128)S(1)} %copy.79) | copy-start | bytes 6148
  453.5 1.3 copy-start.9
  524.5 8.4 %copy-start.8 = (s32[64,8]{0,1:T(8,128)S(1)}, s32[64,8]{0,1:T(8,128)}, u32[]{:S(2)}) copy-start(s32[64,8]{0,1:T(8,128)} %param.22) | copy-start | bytes 6148
  524.5 8.5 %copy-start.5 = (s32[64,8]{1,0:T(8,128)S(1)}, s32[64,8]{1,0:T(8,128)}, u32[]{:S(2)}) copy-start(s32[64,8]{1,0:T(8,128)} %copy-done.4) | copy-start | bytes 6148
  526.9 39.3 %copy-start.2 = (bf16[64,1024]{1,0:T(8,128)(2,1)S(1)}, bf16[64,1024]{1,0:T(8,128)(2,1)}, u32[]{:S(2)}) copy-start(bf16[64,1024]{1,0:T(8,128)(2,1)} %reduce-scatter.2.cloned.1.call-done) | copy-start | bytes 393220
  526.9 35.7 %all-to-all-start.5 = ((bf16[8,16,5,1024]{3,1,2,0:T(8,128)(2,1)}), bf16[8,16,5,1024]{3,1,2,0:T(8,128)(2,1)}, u32[]{:S(2)}, u32[]{:S(2)}) async-start(bf16[8,16,5,1024]{3,1,2,0:T(8,128)(2,1)} %copy.86), calls=%async_computation.6 | async-start | bytes 2621440 | tf_op jit(solution)/shard_map/all_to_all | solution.py:208
Sparse Core Ops, SparseCore 0:
  47.9 84.4 all-gather.2
  135.6 84.5 all-gather.4
  296.4 39.4 reduce-scatter.1
